TPU v7x, 32 devices: a whole 2x2x4 slice. The times are simulated.
32 devices in a mesh: samp: 8 (over z, core), chan: 4 (over y, x).
Axes of the slice: x: 2, y: 2, z: 4, core: 2. Of those that a mesh axis runs over, the one named last changes fastest.
Arguments:
- out_cot: bfloat16 [8, 256, 4096], P('samp', 'chan'), may hold values from -6 to 6
- mix_weight: bfloat16 [256, 256], replicated, may hold values from -0.375 to 0.375
- corr_kernels: float32 [2, 12, 256, 64], P(None, None, 'chan'), may hold values from -0.75 to 0.75
- momentum: int32 [8], P('samp'), may hold values from 0 to 11
- spin_up: int32 [8, 4096], P('samp', 'chan'), may hold values 0 or 1
- layer_input: bfloat16 [8, 256, 4096], P('samp', None, 'chan'), may hold values from -6 to 6
- pre_one: bfloat16 [8, 256, 4096], P('samp', None, 'chan'), may hold values from -6 to 6
- pre_two: bfloat16 [8, 256, 4096], P('samp', None, 'chan'), may hold values from -6 to 6
- conv_weight: bfloat16 [3, 9, 256, 256], replicated, may hold values from -0.125 to 0.125
- dilation: int32 [3, 256], replicated, may hold values from 1 to 4, as said below
Outputs:
- input_grad: bfloat16 [8, 256, 4096], P('samp', None, 'chan')
- weight_grad: float32 [3, 9, 256, 256], P(None, None, 'chan')
Inputs may be any that keep to these rules, and one draw needn't show every extreme that they name: Some channel of every convolution has dilation 4.
All inputs are finite; a program needn't handle non-finite values. No bound on the sum of `spin_up` on one device may be relied on, other than what follows from the above.
Results may differ from a plain program's by a relative error of at most 0.02.
Values may be sent and summed in bfloat16 or wider, within the bound.
A program may use at most 64 MiB of HBM per device.

v0:
```python
import math
import jax
import jax.numpy as jnp
from jax import lax
from jax.sharding import PartitionSpec as P

SIDE = 64
LAYERS = 3
MAXDIL = 4


def with_halo(shard, sides, width):
    for axis, dim in sides:
        size, length = (lax.axis_size(axis), shard.shape[dim])
        up = [(i, (i + 1) % size) for i in range(size)]
        down = [(j, i) for i, j in up]
        last = lax.slice_in_dim(shard, length - width, length, axis=dim)
        leading = lax.slice_in_dim(shard, 0, width, axis=dim)
        before = lax.ppermute(last, axis, up)
        after = lax.ppermute(leading, axis, down)
        shard = jnp.concatenate([before, shard, after], axis=dim)
    return shard


def column_shift(values, step_size, lattice_side, column):
    if step_size == 0:
        return values
    inside = (column - step_size >= 0) & (column - step_size < lattice_side)
    wrapped = step_size - lattice_side if step_size > 0 else step_size + lattice_side
    return jnp.where(inside, jnp.roll(values, step_size, axis=2), jnp.roll(values, wrapped, axis=2))


def on_device(
    out_cot,
    mix_weight,
    corr_kernels,
    momentum,
    spin_up,
    layer_input,
    pre_one,
    pre_two,
    conv_weight,
    dilation,
):
    highest = lax.Precision.HIGHEST
    sample_count = out_cot.shape[0]
    chan_block = out_cot.shape[1]
    site_count = out_cot.shape[2]
    sectors = corr_kernels.shape[1]
    lattice_side = corr_kernels.shape[3]
    slab_cells = layer_input.shape[2]
    own_start = lax.axis_index("chan") * chan_block
    own_rows = lax.dynamic_slice_in_dim(mix_weight, own_start, chan_block, 0)
    input_cot = lax.psum_scatter(
        jnp.einsum("oc,son->csn", own_rows, out_cot, preferred_element_type=jnp.float32),
        "chan",
        scatter_dimension=0,
        tiled=True,
    )
    onehot = (momentum[:, None] == jnp.arange(sectors, dtype=jnp.int32)[None, :]).astype(
        jnp.float32
    )
    picked = jnp.einsum("sk,akci->acsi", onehot, corr_kernels, precision=highest)
    positions = jnp.arange(lattice_side, dtype=jnp.int32)
    circ_table = (
        (positions[None, None, :] - positions[None, :, None]) % lattice_side
        == positions[:, None, None]
    ).astype(jnp.float32)
    circulant = jnp.einsum("acsi,ixy->acsxy", picked, circ_table, precision=highest)
    grid_values = input_cot.reshape(chan_block, sample_count, lattice_side, lattice_side)
    halfway = jnp.einsum("csxX,csxy->csXy", circulant[0], grid_values, precision=highest)
    corr_grad = jnp.einsum("csXy,csyY->scXY", halfway, circulant[1], precision=highest)
    corr_grad = corr_grad.reshape(sample_count, chan_block, site_count).astype(jnp.bfloat16)
    regrouped = lax.all_to_all(corr_grad, "chan", split_axis=2, concat_axis=1, tiled=True)
    spin_gate = jnp.where(spin_up == 1, 1.5, 0.5).astype(jnp.float32)[:, None, :]
    grad_now = (regrouped.astype(jnp.float32) * spin_gate).astype(jnp.bfloat16)
    halo_cells = MAXDIL * SIDE
    column = jnp.arange(slab_cells, dtype=jnp.int32) % lattice_side
    norm_factor = 1.0 / math.sqrt(sample_count * lax.axis_size("samp") * site_count)
    layer_grads = [None] * LAYERS
    input_grad = None
    for conv_level in range(LAYERS - 1, -1, -1):
        slope_base = None
        if conv_level == 0:
            layer_values = layer_input
        else:
            saved_pre = pre_one if conv_level == 1 else pre_two
            slope_base = jnp.tanh(saved_pre.astype(jnp.float32))
            layer_values = slope_base.astype(jnp.bfloat16)
        padded = with_halo(grad_now, (("chan", 2),), halo_cells)
        back_sum = jnp.zeros(grad_now.shape, jnp.float32)
        tap_grads = []
        for row_step in (-1, 0, 1):
            for col_step in (-1, 0, 1):
                tap_index = (row_step + 1) * 3 + col_step + 1
                if row_step == 0 and col_step == 0:
                    combined = grad_now
                else:
                    combined = None
                    for dilate in range(1, MAXDIL + 1):
                        slice_begin = halo_cells - row_step * dilate * lattice_side
                        shifted = column_shift(
                            padded[:, :, slice_begin : slice_begin + slab_cells],
                            col_step * dilate,
                            lattice_side,
                            column,
                        )
                        if combined is None:
                            combined = shifted
                        else:
                            chosen_mask = (dilation[conv_level] == dilate)[None, :, None]
                            combined = jnp.where(chosen_mask, shifted, combined)
                back_sum = back_sum + jnp.einsum(
                    "oc,son->scn",
                    conv_weight[conv_level, tap_index],
                    combined,
                    preferred_element_type=jnp.float32,
                )
                tap_grads.append(
                    jnp.einsum(
                        "son,scn->oc", combined, layer_values, preferred_element_type=jnp.float32
                    )
                    * norm_factor
                )
        local_grad = jnp.stack(tap_grads)
        reduced = lax.psum_scatter(
            local_grad.astype(jnp.bfloat16), "chan", scatter_dimension=1, tiled=True
        )
        layer_grads[conv_level] = lax.psum(reduced, "samp").astype(jnp.float32)
        if conv_level > 0:
            grad_now = (back_sum * (1.0 - slope_base * slope_base)).astype(jnp.bfloat16)
        else:
            input_grad = back_sum.astype(jnp.bfloat16)
    weight_grad = jnp.stack(layer_grads)
    return (input_grad, weight_grad)


def solution(mesh):
    in_specs = (
        P("samp", "chan", None),
        P(),
        P(None, None, "chan", None),
        P("samp"),
        P("samp", "chan"),
        P("samp", None, "chan"),
        P("samp", None, "chan"),
        P("samp", None, "chan"),
        P(),
        P(),
    )
    out_specs = (P("samp", None, "chan"), P(None, None, "chan", None))
    return jax.shard_map(
        on_device, mesh=mesh, in_specs=in_specs, out_specs=out_specs, check_vma=False
    )
```

profile of v0, /device:TPU:0, one launch (start us, length us, event | category | flops | bytes accessed | tf_op | source)
XLA Modules:
  0.0 344.3 jit_solution(6769106226334867354)
XLA Ops:
  7.2 3.8 %convolution_bitcast_fusion = f32[256,1,4096]{2,0,1:T(8,128)} fusion(bf16[1,64,4096]{2,1,0:T(8,128)(2,1)} %param.10, bf16[256,256]{1,0:T(8,128)(2,1)} %param.11, s32[]{:T(128)S(6)} %select_n.3285), kind=kOutput, calls=%fused_computation | convolution fusion | flops 134217728 | bytes 4751364 | tf_op jit(solution)/shard_map/oc,son->csn/dot_general | solution.py:55
  12.7 1.8 fusion.5
  14.5 2.3 slice_bitcast_fusion
  16.8 49.8 %reduce-scatter.5.cloned.1.call-done = f32[64,1,4096]{2,0,1:T(8,128)} async-done(((f32[256,1,4096]{2,0,1:T(8,128)}), f32[64,1,4096]{2,0,1:T(8,128)}) %reduce-scatter.5.cloned.1.call-update) | async-done | bytes 1048592 | tf_op jit(solution)/shard_map/reduce_scatter | solution.py:54
  66.7 2.2 reshape.16731
  68.8 6.2 %fusion.2 = f32[64,64,64]{2,1,0:T(8,128)S(1)} fusion(f32[64,64,64]{2,1,0:T(8,128)S(1)} %reshape.16731, f32[64,64,64]{2,0,1:T(8,128)} %get-tuple-element.25), kind=kOutput, calls=%fused_computation.119 | convolution fusion | flops 201326592 | bytes 3145728 | tf_op jit(solution)/shard_map/csxX,csxy->csXy/dot_general | solution.py:71
  75.0 3.3 fusion.7
  79.2 2.8 copy.42
  82.5 23.6 %reduce.18 = bf16[4096,64]{1,0:T(8,128)(2,1)} reduce(bf16[4096,1,64]{2,1,0:T(2,128)(2,1)S(1)} %bitcast.976, bf16[]{:T(256)} %broadcast.4323), dimensions={1}, to_apply=%bitcast.918.reduce_sub_computation | reduce | bytes 1048578
  106.1 2.7 reshape.16776
  108.7 3.5 %all-to-all-start = ((bf16[4,2,32768]{2,1,0:T(2,128)(2,1)}), bf16[4,2,32768]{2,1,0:T(2,128)(2,1)S(1)}, u32[]{:S(2)}, u32[]{:S(2)}) async-start(bf16[4,2,32768]{2,1,0:T(2,128)(2,1)} %reshape.16776), calls=%async_computation.1 | async-start | bytes 1048576 | tf_op jit(solution)/shard_map/all_to_all | solution.py:74
  114.4 6.1 %all-to-all-done = bf16[4,2,32768]{2,1,0:T(2,128)(2,1)S(1)} async-done(((bf16[4,2,32768]{2,1,0:T(2,128)(2,1)}), bf16[4,2,32768]{2,1,0:T(2,128)(2,1)S(1)}, u32[]{:S(2)}, u32[]{:S(2)}) %all-to-all-start) | async-done | bytes 524320 | tf_op jit(solution)/shard_map/all_to_all | solution.py:74
  121.3 2.3 copy.43
  126.2 1.5 collective-permute-start.1
  127.7 1.9 collective-permute-start
  129.6 4.8 %collective-permute-done = bf16[1,256,256]{1,2,0:T(8,128)(2,1)S(1)} collective-permute-done((bf16[1,256,256]{1,2,0:T(8,128)(2,1)S(1)}, bf16[1,256,256]{1,2,0:T(8,128)(2,1)S(1)}, u32[]{:S(2)}, u32[]{:S(2)}) %collective-permute-start) | collective-permute-done | bytes 131104 | tf_op jit(solution)/shard_map/ppermute | solution.py:20
  137.4 3.0 fusion.252
  142.1 1.2 convolution_add_fusion.23
  143.4 3.0 fusion.256
  146.4 1.2 convolution_add_fusion.22
  147.6 3.0 fusion.260
  150.6 1.2 convolution_add_fusion.21
  151.8 1.3 convolution_add_fusion.20
  153.1 3.0 fusion.264
  156.1 1.2 convolution_add_fusion.19
  157.4 3.0 fusion.268
  160.4 1.2 convolution_add_fusion.18
  161.6 1.2 convolution_add_fusion.17
  162.9 3.0 fusion.272
  165.9 1.2 fusion.14
  168.8 2.0 collective-permute-start.2
  177.7 3.0 fusion.276
  182.4 1.2 convolution_add_fusion.15
  183.7 3.0 fusion.280
  186.7 1.2 convolution_add_fusion.14
  187.9 3.0 fusion.284
  190.9 1.2 convolution_add_fusion.13
  192.2 1.2 convolution_add_fusion.12
  193.4 3.0 fusion.288
  196.4 1.2 convolution_add_fusion.11
  197.6 3.0 fusion.292
  200.7 1.2 convolution_add_fusion.10
  201.9 1.2 convolution_add_fusion.9
  203.1 3.0 fusion.296
  206.2 1.2 fusion.15
  208.5 2.0 collective-permute-start.4
  218.1 3.0 fusion.300
  223.8 3.0 fusion.304
  227.8 3.0 fusion.308
  232.9 3.0 fusion.312
  236.8 3.0 fusion.316
  241.9 3.0 fusion.320
  245.9 1.2 fusion.435
  247.1 1.2 convolution_add_fusion.7
  248.3 1.2 convolution_add_fusion.6
  249.6 1.3 convolution_add_fusion.5
  250.8 1.3 convolution_add_fusion.4
  252.1 1.2 convolution_add_fusion.3
  253.4 1.3 convolution_add_fusion.2
  254.7 20.1 %reduce-scatter.7.cloned.1.call-done = bf16[9,64,256]{2,1,0:T(8,128)(2,1)} async-done(((bf16[9,256,256]{2,1,0:T(8,128)(2,1)}), bf16[9,64,256]{2,1,0:T(8,128)(2,1)}) %reduce-scatter.7.cloned.1.call-update) | async-done | bytes 294928 | tf_op jit(solution)/shard_map/reduce_scatter | solution.py:126
  274.9 1.2 convolution_add_fusion.1
  276.1 1.3 fusion.17
  278.4 56.7 %all-reduce.3.cloned.1.call-done = (bf16[1,9,64,256]{3,2,1,0:T(8,128)(2,1)}, bf16[1,9,64,256]{3,2,1,0:T(8,128)(2,1)}, bf16[1,9,64,256]{3,2,1,0:T(8,128)(2,1)}) async-done(((bf16[1,9,64,256]{3,2,1,0:T(8,128)(2,1)}, bf16[1,9,64,256]{3,2,1,0:T(8,128)(2,1)}, bf16[1,9,64,256]{3,2,1,0:T(8,128)(2,1)}), (bf16[1,9,64,256]{3,2,1,0:T(8,128)(2,1)}, bf16[1,9,64,256]{3,2,1,0:T(8,128)(2,1)}, ...) | async-done | bytes 884752 | tf_op jit(solution)/shard_map/psum | solution.py:129
  335.0 2.5 maximum_convert_fusion
  (210 shorter events, 41.9 us)
Async XLA Ops:
  7.2 4.7 %copy-start = (f32[2,12,64,64]{3,2,1,0:T(8,128)S(1)}, f32[2,12,64,64]{3,2,1,0:T(8,128)}, u32[]{:S(2)}) copy-start(f32[2,12,64,64]{3,2,1,0:T(8,128)} %param.12) | copy-start | bytes 1179652
  7.2 59.5 %reduce-scatter.5.cloned.1.call-start = ((), (), s32[]{:S(2)}) async-start(), calls=%async_computation.5 | async-start | bytes 5242880 | tf_op jit(solution)/shard_map/reduce_scatter | solution.py:54
  68.8 6.2 %copy-start.2 = (f32[64,64,64]{2,0,1:T(8,128)S(1)}, f32[64,64,64]{2,0,1:T(8,128)}, u32[]{:S(2)}) copy-start(f32[64,64,64]{2,0,1:T(8,128)} %get-tuple-element.24) | copy-start | bytes 3145732
  106.1 6.2 %copy-start.15 = (bf16[1,256,1024]{2,1,0:T(8,128)(2,1)S(1)}, bf16[1,256,1024]{2,1,0:T(8,128)(2,1)}, u32[]{:S(2)}) copy-start(bf16[1,256,1024]{2,1,0:T(8,128)(2,1)} %param.16) | copy-start | bytes 1572868
  106.1 7.2 %copy-start.16 = (bf16[1,256,1024]{2,1,0:T(8,128)(2,1)S(1)}, bf16[1,256,1024]{2,1,0:T(8,128)(2,1)}, u32[]{:S(2)}) copy-start(bf16[1,256,1024]{2,1,0:T(8,128)(2,1)} %param.17) | copy-start | bytes 1572868
  106.1 8.2 %copy-start.18 = (s32[3,256]{1,0:T(4,128)S(1)}, s32[3,256]{1,0:T(4,128)}, u32[]{:S(2)}) copy-start(s32[3,256]{1,0:T(4,128)} %param.19) | copy-start | bytes 9220
  106.1 8.3 %copy-start.17 = (s32[1,1024]{1,0:T(1,128)S(1)}, s32[1,1024]{1,0:T(1,128)}, u32[]{:S(2)}) copy-start(s32[1,1024]{1,0:T(1,128)} %param.14) | copy-start | bytes 12292
  108.7 11.7 %all-to-all-start = ((bf16[4,2,32768]{2,1,0:T(2,128)(2,1)}), bf16[4,2,32768]{2,1,0:T(2,128)(2,1)S(1)}, u32[]{:S(2)}, u32[]{:S(2)}) async-start(bf16[4,2,32768]{2,1,0:T(2,128)(2,1)} %reshape.16776), calls=%async_computation.1 | async-start | bytes 1048576 | tf_op jit(solution)/shard_map/all_to_all | solution.py:74
  112.2 142.5 %reduce-scatter.11.cloned.1.call-start = ((), (), s32[]{:S(2)}) async-start(), calls=%async_computation.8 | async-start | bytes 1474560 | tf_op jit(solution)/shard_map/reduce_scatter | solution.py:126
  126.2 8.3 %collective-permute-start.1 = (bf16[1,256,256]{1,2,0:T(8,128)(2,1)S(1)}, bf16[1,256,256]{1,2,0:T(8,128)(2,1)S(1)}, u32[]{:S(2)}, u32[]{:S(2)}) collective-permute-start(bf16[1,256,256]{1,2,0:T(8,128)(2,1)S(1)} %get-tuple-element.324), channel_id=1, source_target_pairs={{0,1},{1,2},{2,3},{3,0},{4,5},{5,6},{6,7},{7,4},{8,9},{9,10},{10,1... | collective-permute-start | bytes 393224 | tf_op jit(solution)/shard_map/ppermute | solution.py:19
  127.7 6.7 %collective-permute-start = (bf16[1,256,256]{1,2,0:T(8,128)(2,1)S(1)}, bf16[1,256,256]{1,2,0:T(8,128)(2,1)S(1)}, u32[]{:S(2)}, u32[]{:S(2)}) collective-permute-start(bf16[1,256,256]{1,2,0:T(8,128)(2,1)S(1)} %get-tuple-element.325), channel_id=1, source_target_pairs={{1,0},{2,1},{3,2},{0,3},{5,4},{6,5},{7,6},{4,7},{9,8},{10,9},{11,1... | collective-permute-start | bytes 393224 | tf_op jit(solution)/shard_map/ppermute | solution.py:20
  162.9 3.0 copy-start.8
  167.7 7.3 %collective-permute-start.3 = (bf16[1,256,256]{1,2,0:T(8,128)(2,1)S(1)}, bf16[1,256,256]{1,2,0:T(8,128)(2,1)S(1)}, u32[]{:S(2)}, u32[]{:S(2)}) collective-permute-start(bf16[1,256,256]{1,2,0:T(8,128)(2,1)S(1)} %get-tuple-element.258), channel_id=1, source_target_pairs={{0,1},{1,2},{2,3},{3,0},{4,5},{5,6},{6,7},{7,4},{8,9},{9,10},{10,1... | collective-permute-start | bytes 393224 | tf_op jit(solution)/shard_map/ppermute | solution.py:19
  168.8 6.1 %collective-permute-start.2 = (bf16[1,256,256]{1,2,0:T(8,128)(2,1)S(1)}, bf16[1,256,256]{1,2,0:T(8,128)(2,1)S(1)}, u32[]{:S(2)}, u32[]{:S(2)}) collective-permute-start(bf16[1,256,256]{1,2,0:T(8,128)(2,1)S(1)} %get-tuple-element.259), channel_id=1, source_target_pairs={{1,0},{2,1},{3,2},{0,3},{5,4},{6,5},{7,6},{4,7},{9,8},{10,9},{11,1... | collective-permute-start | bytes 393224 | tf_op jit(solution)/shard_map/ppermute | solution.py:20
  173.8 1.0 copy-start.13
  174.8 79.9 %reduce-scatter.9.cloned.1.call-start = ((), (), s32[]{:S(2)}) async-start(), calls=%async_computation.7 | async-start | bytes 1474560 | tf_op jit(solution)/shard_map/reduce_scatter | solution.py:126
  203.1 3.0 copy-start.7
  207.6 7.8 %collective-permute-start.5 = (bf16[1,256,256]{1,2,0:T(8,128)(2,1)S(1)}, bf16[1,256,256]{1,2,0:T(8,128)(2,1)S(1)}, u32[]{:S(2)}, u32[]{:S(2)}) collective-permute-start(bf16[1,256,256]{1,2,0:T(8,128)(2,1)S(1)} %get-tuple-element.192), channel_id=1, source_target_pairs={{0,1},{1,2},{2,3},{3,0},{4,5},{5,6},{6,7},{7,4},{8,9},{9,10},{10,1... | collective-permute-start | bytes 393224 | tf_op jit(solution)/shard_map/ppermute | solution.py:19
  208.5 6.8 %collective-permute-start.4 = (bf16[1,256,256]{1,2,0:T(8,128)(2,1)S(1)}, bf16[1,256,256]{1,2,0:T(8,128)(2,1)S(1)}, u32[]{:S(2)}, u32[]{:S(2)}) collective-permute-start(bf16[1,256,256]{1,2,0:T(8,128)(2,1)S(1)} %get-tuple-element.193), channel_id=1, source_target_pairs={{1,0},{2,1},{3,2},{0,3},{5,4},{6,5},{7,6},{4,7},{9,8},{10,9},{11,1... | collective-permute-start | bytes 393224 | tf_op jit(solution)/shard_map/ppermute | solution.py:20
  213.9 1.0 copy-start.14
  215.0 59.8 %reduce-scatter.7.cloned.1.call-start = ((), (), s32[]{:S(2)}) async-start(), calls=%async_computation.6 | async-start | bytes 1474560 | tf_op jit(solution)/shard_map/reduce_scatter | solution.py:126
  218.1 3.0 copy-start.19
  222.7 4.1 %copy-start.11 = (bf16[256,1024]{0,1:T(8,128)(2,1)}, bf16[256,1024]{0,1:T(8,128)(2,1)S(1)}, u32[]{:S(2)}) copy-start(bf16[256,1024]{0,1:T(8,128)(2,1)S(1)} %get-tuple-element.123) | copy-start | bytes 1572868
  222.7 18.2 %copy-start.9 = (bf16[256,1024]{0,1:T(8,128)(2,1)}, bf16[256,1024]{0,1:T(8,128)(2,1)S(1)}, u32[]{:S(2)}) copy-start(bf16[256,1024]{0,1:T(8,128)(2,1)S(1)} %get-tuple-element.122) | copy-start | bytes 1572868
  235.8 4.0 %copy-start.3 = (bf16[256,1024]{0,1:T(8,128)(2,1)}, bf16[256,1024]{0,1:T(8,128)(2,1)S(1)}, u32[]{:S(2)}) copy-start(bf16[256,1024]{0,1:T(8,128)(2,1)S(1)} %fusion.312) | copy-start | bytes 1572868
  239.8 2.0 copy-start.5
  244.8 2.3 copy-start.12
  245.9 89.1 %all-reduce.3.cloned.1.call-start = ((), (), s32[]{:S(2)}) async-start(), calls=%async_computation.9 | async-start | bytes 1769472 | tf_op jit(solution)/shard_map/psum | solution.py:129
  249.6 2.6 copy-start.4
  250.8 2.5 copy-start.6
  253.4 21.5 %copy-start.10 = (bf16[256,1024]{0,1:T(8,128)(2,1)S(1)}, bf16[256,1024]{0,1:T(8,128)(2,1)}, u32[]{:S(2)}) copy-start(bf16[256,1024]{0,1:T(8,128)(2,1)} %copy-done.9) | copy-start | bytes 1572868
  276.1 61.5 %copy-start.1 = (f32[2,12,64,64]{3,2,1,0:T(8,128)S(1)}, f32[2,12,64,64]{3,2,1,0:T(8,128)}, u32[]{:S(2)}) copy-start(f32[2,12,64,64]{3,2,1,0:T(8,128)} %param.12) | copy-start | bytes 1179652
Sparse Core Ops, SparseCore 0:
  11.2 55.3 reduce-scatter.4
  174.9 27.8 reduce-scatter.10
  215.1 28.0 reduce-scatter.8
  246.3 28.5 reduce-scatter.6
  277.4 57.5 all-reduce.2
where the time goes:
time: 348 us; the launch traced here: 344 us
  waiting for transfers between devices  138 us (40%)
  other arithmetic  90.3 us (26%)
  matrix products  64.6 us (19%)
  local copies, waits for them, and re-layouts  22.2 us (6%)
  between operations  16.2 us (5%)
  starting transfers between devices  13.4 us (4%)
    psum x1, waiting for transfers between devices, on_device(): layer_grads[conv_level] = lax.psum(reduced, 'samp').astype(jnp.float32)  56.7 us
    select_n x18, other arithmetic, on_device(): combined = jnp.where(chosen_mask, shifted, combined)  54 us
    reduce_scatter x1, waiting for transfers between devices, on_device(): lax.psum_scatter(jnp.einsum('oc,son->csn', own_rows, out_cot, preferred_e...  49.8 us
    dot_general x27, matrix products, on_device(): jnp.einsum('oc,son->scn', conv_weight[conv_level, tap_index], combined, p...  32.9 us
    unnamed x1, other arithmetic  23.6 us
    reduce_scatter x3, waiting for transfers between devices, on_device(): lax.psum_scatter(local_grad.astype(jnp.bfloat16), 'chan', scatter_dimensi...  20.1 us
    dot_general x27, matrix products, on_device(): jnp.einsum('son,scn->oc', combined, layer_values, preferred_element_type=...  15.7 us
    unnamed x46, local copies, waits for them, and re-layouts  9.22 us
  transfers between devices with their start and end apart: 12, of which 5 were waited for; matrix products, arithmetic and copies ran while one was open for 26% of the time, Pallas kernels for 0%

commit v1 on v0

--- a/solution.py
+++ b/solution.py
@@ -126,7 +126,9 @@
         reduced = lax.psum_scatter(
             local_grad.astype(jnp.bfloat16), "chan", scatter_dimension=1, tiled=True
         )
-        layer_grads[conv_level] = lax.psum(reduced, "samp").astype(jnp.float32)
+        layer_grads[conv_level] = jnp.sum(lax.all_gather(reduced, "samp"), axis=0).astype(
+            jnp.float32
+        )
         if conv_level > 0:
             grad_now = (back_sum * (1.0 - slope_base * slope_base)).astype(jnp.bfloat16)
         else:

time: 348 us -> 388 us (1.11)
  waiting for transfers between devices: 138 us -> 171 us
  other arithmetic: 90.3 us -> 95.5 us
    all_gather x0 -> x3, waiting for transfers between devices: none -> 81.6 us  [on_device(): lax.all_gather(reduced, 'samp')]
    psum x1 -> x0, waiting for transfers between devices: 56.7 us -> none  [on_device(): layer_grads[conv_level] = lax.psum(reduced, 'samp').astype(jnp.float32)]
    reduce_scatter x3, waiting for transfers between devices: 20.1 us -> 27.7 us  [on_device(): lax.psum_scatter(local_grad.astype(jnp.bfloat16), 'chan', scatter_dimensi...]
    reduce_sum x0 -> x3, other arithmetic: none -> 6.4 us  [on_device(): jnp.sum(lax.all_gather(reduced, 'samp'), axis=0).astype(jnp.float32)]
    unnamed x46 -> x40, local copies, waits for them, and re-layouts: 9.22 us -> 9.21 us
  transfers between devices with their start and end apart: 12 -> 14, of which waited for: 5 -> 7; matrix products, arithmetic and copies ran while one was open for 26% -> 24% of each run, Pallas kernels for 0% -> 0%
where the time goes in v1:
time: 388 us; the launch traced here: 384 us
  waiting for transfers between devices  171 us (44%)
  other arithmetic  95.5 us (25%)
  matrix products  64.6 us (17%)
  local copies, waits for them, and re-layouts  22.2 us (6%)
  between operations  16.6 us (4%)
  starting transfers between devices  13.7 us (4%)
    all_gather x3, waiting for transfers between devices, on_device(): lax.all_gather(reduced, 'samp')  81.6 us
    select_n x18, other arithmetic, on_device(): combined = jnp.where(chosen_mask, shifted, combined)  54 us
    reduce_scatter x1, waiting for transfers between devices, on_device(): lax.psum_scatter(jnp.einsum('oc,son->csn', own_rows, out_cot, preferred_e...  49.8 us
    dot_general x27, matrix products, on_device(): jnp.einsum('oc,son->scn', conv_weight[conv_level, tap_index], combined, p...  32.9 us
    reduce_scatter x3, waiting for transfers between devices, on_device(): lax.psum_scatter(local_grad.astype(jnp.bfloat16), 'chan', scatter_dimensi...  27.7 us
    unnamed x1, other arithmetic  23.6 us
    dot_general x27, matrix products, on_device(): jnp.einsum('son,scn->oc', combined, layer_values, preferred_element_type=...  15.7 us
    unnamed x40, local copies, waits for them, and re-layouts  9.21 us
  transfers between devices with their start and end apart: 14, of which 7 were waited for; matrix products, arithmetic and copies ran while one was open for 24% of the time, Pallas kernels for 0%

profile of v1, /device:TPU:0, one launch (start us, length us, event | category | flops | bytes accessed | tf_op | source)
XLA Modules:
  0.0 383.7 jit_solution(12662061163557476276)
XLA Ops:
  7.2 3.8 convolution_bitcast_fusion
  12.7 1.8 fusion.5
  14.5 2.3 slice_bitcast_fusion
  16.8 49.8 %reduce-scatter.5.cloned.1.call-done = f32[64,1,4096]{2,0,1:T(8,128)} async-done(((f32[256,1,4096]{2,0,1:T(8,128)}), f32[64,1,4096]{2,0,1:T(8,128)}) %reduce-scatter.5.cloned.1.call-update) | async-done | bytes 1048592 | tf_op jit(solution)/shard_map/reduce_scatter | solution.py:54
  66.6 2.2 reshape.16758
  68.8 6.2 %fusion.2 = f32[64,64,64]{2,1,0:T(8,128)S(1)} fusion(f32[64,64,64]{2,1,0:T(8,128)S(1)} %reshape.16758, f32[64,64,64]{2,0,1:T(8,128)} %get-tuple-element.22), kind=kOutput, calls=%fused_computation.119 | convolution fusion | flops 201326592 | bytes 3145728 | tf_op jit(solution)/shard_map/csxX,csxy->csXy/dot_general | solution.py:71
  75.0 3.3 fusion.7
  79.1 2.8 copy.42
  82.4 23.6 %reduce.21 = bf16[4096,64]{1,0:T(8,128)(2,1)} reduce(bf16[4096,1,64]{2,1,0:T(2,128)(2,1)S(1)} %bitcast.979, bf16[]{:T(256)} %broadcast.4323), dimensions={1}, to_apply=%bitcast.921.reduce_sub_computation | reduce | bytes 1048578
  106.0 2.7 reshape.16806
  108.7 3.5 all-to-all-start
  114.3 6.1 %all-to-all-done = bf16[4,2,32768]{2,1,0:T(2,128)(2,1)S(1)} async-done(((bf16[4,2,32768]{2,1,0:T(2,128)(2,1)}), bf16[4,2,32768]{2,1,0:T(2,128)(2,1)S(1)}, u32[]{:S(2)}, u32[]{:S(2)}) %all-to-all-start) | async-done | bytes 524320 | tf_op jit(solution)/shard_map/all_to_all | solution.py:74
  121.3 2.3 copy.43
  126.2 1.5 collective-permute-start.1
  127.7 1.9 collective-permute-start
  129.6 4.8 %collective-permute-done = bf16[1,256,256]{1,2,0:T(8,128)(2,1)S(1)} collective-permute-done((bf16[1,256,256]{1,2,0:T(8,128)(2,1)S(1)}, bf16[1,256,256]{1,2,0:T(8,128)(2,1)S(1)}, u32[]{:S(2)}, u32[]{:S(2)}) %collective-permute-start) | collective-permute-done | bytes 131104 | tf_op jit(solution)/shard_map/ppermute | solution.py:20
  137.4 3.0 fusion.252
  140.5 1.2 fusion.455
  142.2 1.2 convolution_add_fusion.23
  143.4 3.0 fusion.256
  147.6 3.0 fusion.260
  151.9 1.3 convolution_add_fusion.20
  153.1 3.0 fusion.264
  156.1 1.2 convolution_add_fusion.19
  157.4 3.0 fusion.268
  160.4 1.2 convolution_add_fusion.18
  161.6 1.2 convolution_add_fusion.17
  162.9 3.0 fusion.272
  165.9 1.2 fusion.14
  168.9 2.0 collective-permute-start.2
  177.8 3.0 fusion.276
  182.5 1.2 convolution_add_fusion.15
  183.8 3.0 fusion.280
  186.8 1.2 convolution_add_fusion.14
  188.0 3.0 fusion.284
  191.0 1.2 convolution_add_fusion.13
  192.2 1.2 convolution_add_fusion.12
  193.5 3.0 fusion.288
  196.5 1.2 convolution_add_fusion.11
  197.7 3.0 fusion.292
  200.7 1.2 convolution_add_fusion.10
  203.2 3.0 fusion.296
  206.2 1.2 fusion.15
  208.6 2.2 collective-permute-start.4
  218.2 3.0 fusion.300
  223.8 3.0 fusion.304
  227.8 3.0 fusion.308
  232.9 3.0 fusion.312
  236.9 3.0 fusion.316
  241.9 3.0 fusion.320
  247.3 27.7 %reduce-scatter.7.cloned.1.call-done = bf16[9,64,256]{2,1,0:T(8,128)(2,1)} async-done(((bf16[9,256,256]{2,1,0:T(8,128)(2,1)}), bf16[9,64,256]{2,1,0:T(8,128)(2,1)}) %reduce-scatter.7.cloned.1.call-update) | async-done | bytes 294928 | tf_op jit(solution)/shard_map/reduce_scatter | solution.py:126
  276.2 1.4 convolution_add_fusion.7
  280.0 1.3 convolution_add_fusion.4
  281.3 1.3 convolution_add_fusion.3
  282.6 1.2 convolution_add_fusion.2
  283.8 1.2 convolution_add_fusion.1
  285.0 1.2 fusion.17
  287.2 21.0 %all-gather.11.cloned.1.call-done = bf16[72,64,256]{2,1,0:T(8,128)(2,1)} async-done(((bf16[9,64,256]{2,1,0:T(8,128)(2,1)}), bf16[72,64,256]{2,1,0:T(8,128)(2,1)}) %all-gather.11.cloned.1.call-update) | async-done | bytes 2359312 | tf_op jit(solution)/shard_map/all_gather | solution.py:129
  308.2 2.1 reduce_sum.38
  310.3 30.2 %all-gather.9.cloned.1.call-done = bf16[72,64,256]{2,1,0:T(8,128)(2,1)} async-done(((bf16[9,64,256]{2,1,0:T(8,128)(2,1)}), bf16[72,64,256]{2,1,0:T(8,128)(2,1)}) %all-gather.9.cloned.1.call-update) | async-done | bytes 2359312 | tf_op jit(solution)/shard_map/all_gather | solution.py:129
  340.6 2.1 reduce_sum.37
  342.7 30.4 %all-gather.7.cloned.1.call-done = bf16[72,64,256]{2,1,0:T(8,128)(2,1)} async-done(((bf16[9,64,256]{2,1,0:T(8,128)(2,1)}), bf16[72,64,256]{2,1,0:T(8,128)(2,1)}) %all-gather.7.cloned.1.call-update) | async-done | bytes 2359312 | tf_op jit(solution)/shard_map/all_gather | solution.py:129
  373.1 2.2 reduce_sum.36
  375.3 1.3 maximum_convert_fusion
  (213 shorter events, 48.9 us)
Async XLA Ops:
  7.2 4.6 %copy-start = (f32[2,12,64,64]{3,2,1,0:T(8,128)S(1)}, f32[2,12,64,64]{3,2,1,0:T(8,128)}, u32[]{:S(2)}) copy-start(f32[2,12,64,64]{3,2,1,0:T(8,128)} %param.12) | copy-start | bytes 1179652
  7.2 59.5 %reduce-scatter.5.cloned.1.call-start = ((), (), s32[]{:S(2)}) async-start(), calls=%async_computation.5 | async-start | bytes 5242880 | tf_op jit(solution)/shard_map/reduce_scatter | solution.py:54
  68.8 6.2 %copy-start.2 = (f32[64,64,64]{2,0,1:T(8,128)S(1)}, f32[64,64,64]{2,0,1:T(8,128)}, u32[]{:S(2)}) copy-start(f32[64,64,64]{2,0,1:T(8,128)} %get-tuple-element.21) | copy-start | bytes 3145732
  106.0 6.2 %copy-start.12 = (bf16[1,256,1024]{2,1,0:T(8,128)(2,1)S(1)}, bf16[1,256,1024]{2,1,0:T(8,128)(2,1)}, u32[]{:S(2)}) copy-start(bf16[1,256,1024]{2,1,0:T(8,128)(2,1)} %param.16) | copy-start | bytes 1572868
  106.0 7.2 %copy-start.13 = (bf16[1,256,1024]{2,1,0:T(8,128)(2,1)S(1)}, bf16[1,256,1024]{2,1,0:T(8,128)(2,1)}, u32[]{:S(2)}) copy-start(bf16[1,256,1024]{2,1,0:T(8,128)(2,1)} %param.17) | copy-start | bytes 1572868
  106.0 8.2 %copy-start.15 = (s32[3,256]{1,0:T(4,128)S(1)}, s32[3,256]{1,0:T(4,128)}, u32[]{:S(2)}) copy-start(s32[3,256]{1,0:T(4,128)} %param.19) | copy-start | bytes 9220
  106.0 8.3 %copy-start.14 = (s32[1,1024]{1,0:T(1,128)S(1)}, s32[1,1024]{1,0:T(1,128)}, u32[]{:S(2)}) copy-start(s32[1,1024]{1,0:T(1,128)} %param.14) | copy-start | bytes 12292
  108.7 11.7 %all-to-all-start = ((bf16[4,2,32768]{2,1,0:T(2,128)(2,1)}), bf16[4,2,32768]{2,1,0:T(2,128)(2,1)S(1)}, u32[]{:S(2)}, u32[]{:S(2)}) async-start(bf16[4,2,32768]{2,1,0:T(2,128)(2,1)} %reshape.16806), calls=%async_computation.1 | async-start | bytes 1048576 | tf_op jit(solution)/shard_map/all_to_all | solution.py:74
  112.2 133.7 %reduce-scatter.11.cloned.1.call-start = ((), (), s32[]{:S(2)}) async-start(), calls=%async_computation.8 | async-start | bytes 1474560 | tf_op jit(solution)/shard_map/reduce_scatter | solution.py:126
  126.2 8.3 %collective-permute-start.1 = (bf16[1,256,256]{1,2,0:T(8,128)(2,1)S(1)}, bf16[1,256,256]{1,2,0:T(8,128)(2,1)S(1)}, u32[]{:S(2)}, u32[]{:S(2)}) collective-permute-start(bf16[1,256,256]{1,2,0:T(8,128)(2,1)S(1)} %get-tuple-element.321), channel_id=1, source_target_pairs={{0,1},{1,2},{2,3},{3,0},{4,5},{5,6},{6,7},{7,4},{8,9},{9,10},{10,1... | collective-permute-start | bytes 393224 | tf_op jit(solution)/shard_map/ppermute | solution.py:19
  127.7 6.7 %collective-permute-start = (bf16[1,256,256]{1,2,0:T(8,128)(2,1)S(1)}, bf16[1,256,256]{1,2,0:T(8,128)(2,1)S(1)}, u32[]{:S(2)}, u32[]{:S(2)}) collective-permute-start(bf16[1,256,256]{1,2,0:T(8,128)(2,1)S(1)} %get-tuple-element.322), channel_id=1, source_target_pairs={{1,0},{2,1},{3,2},{0,3},{5,4},{6,5},{7,6},{4,7},{9,8},{10,9},{11,1... | collective-permute-start | bytes 393224 | tf_op jit(solution)/shard_map/ppermute | solution.py:20
  162.9 3.0 copy-start.6
  167.7 7.3 %collective-permute-start.3 = (bf16[1,256,256]{1,2,0:T(8,128)(2,1)S(1)}, bf16[1,256,256]{1,2,0:T(8,128)(2,1)S(1)}, u32[]{:S(2)}, u32[]{:S(2)}) collective-permute-start(bf16[1,256,256]{1,2,0:T(8,128)(2,1)S(1)} %get-tuple-element.255), channel_id=1, source_target_pairs={{0,1},{1,2},{2,3},{3,0},{4,5},{5,6},{6,7},{7,4},{8,9},{9,10},{10,1... | collective-permute-start | bytes 393224 | tf_op jit(solution)/shard_map/ppermute | solution.py:19
  168.9 6.1 %collective-permute-start.2 = (bf16[1,256,256]{1,2,0:T(8,128)(2,1)S(1)}, bf16[1,256,256]{1,2,0:T(8,128)(2,1)S(1)}, u32[]{:S(2)}, u32[]{:S(2)}) collective-permute-start(bf16[1,256,256]{1,2,0:T(8,128)(2,1)S(1)} %get-tuple-element.256), channel_id=1, source_target_pairs={{1,0},{2,1},{3,2},{0,3},{5,4},{6,5},{7,6},{4,7},{9,8},{10,9},{11,1... | collective-permute-start | bytes 393224 | tf_op jit(solution)/shard_map/ppermute | solution.py:20
  173.8 1.0 copy-start.10
  174.9 71.6 %reduce-scatter.9.cloned.1.call-start = ((), (), s32[]{:S(2)}) async-start(), calls=%async_computation.7 | async-start | bytes 1474560 | tf_op jit(solution)/shard_map/reduce_scatter | solution.py:126
  203.2 3.0 copy-start.5
  207.7 7.8 %collective-permute-start.5 = (bf16[1,256,256]{1,2,0:T(8,128)(2,1)S(1)}, bf16[1,256,256]{1,2,0:T(8,128)(2,1)S(1)}, u32[]{:S(2)}, u32[]{:S(2)}) collective-permute-start(bf16[1,256,256]{1,2,0:T(8,128)(2,1)S(1)} %get-tuple-element.189), channel_id=1, source_target_pairs={{0,1},{1,2},{2,3},{3,0},{4,5},{5,6},{6,7},{7,4},{8,9},{9,10},{10,1... | collective-permute-start | bytes 393224 | tf_op jit(solution)/shard_map/ppermute | solution.py:19
  208.6 6.8 %collective-permute-start.4 = (bf16[1,256,256]{1,2,0:T(8,128)(2,1)S(1)}, bf16[1,256,256]{1,2,0:T(8,128)(2,1)S(1)}, u32[]{:S(2)}, u32[]{:S(2)}) collective-permute-start(bf16[1,256,256]{1,2,0:T(8,128)(2,1)S(1)} %get-tuple-element.190), channel_id=1, source_target_pairs={{1,0},{2,1},{3,2},{0,3},{5,4},{6,5},{7,6},{4,7},{9,8},{10,9},{11,1... | collective-permute-start | bytes 393224 | tf_op jit(solution)/shard_map/ppermute | solution.py:20
  214.2 1.1 copy-start.11
  215.3 59.7 %reduce-scatter.7.cloned.1.call-start = ((), (), s32[]{:S(2)}) async-start(), calls=%async_computation.6 | async-start | bytes 1474560 | tf_op jit(solution)/shard_map/reduce_scatter | solution.py:126
  218.2 3.0 copy-start.16
  222.7 4.1 %copy-start.9 = (bf16[256,1024]{0,1:T(8,128)(2,1)}, bf16[256,1024]{0,1:T(8,128)(2,1)S(1)}, u32[]{:S(2)}) copy-start(bf16[256,1024]{0,1:T(8,128)(2,1)S(1)} %get-tuple-element.120) | copy-start | bytes 1572868
  222.7 18.1 %copy-start.7 = (bf16[256,1024]{0,1:T(8,128)(2,1)}, bf16[256,1024]{0,1:T(8,128)(2,1)S(1)}, u32[]{:S(2)}) copy-start(bf16[256,1024]{0,1:T(8,128)(2,1)S(1)} %get-tuple-element.119) | copy-start | bytes 1572868
  239.9 2.0 copy-start.3
  245.9 62.4 %all-gather.11.cloned.1.call-start = ((), (), s32[]{:S(2)}) async-start(), calls=%async_computation.11 | async-start | bytes 2654208 | tf_op jit(solution)/shard_map/all_gather | solution.py:129
  246.4 94.1 %all-gather.9.cloned.1.call-start = ((), (), s32[]{:S(2)}) async-start(), calls=%async_computation.10 | async-start | bytes 2654208 | tf_op jit(solution)/shard_map/all_gather | solution.py:129
  247.0 126.1 %all-gather.7.cloned.1.call-start = ((), (), s32[]{:S(2)}) async-start(), calls=%async_computation.9 | async-start | bytes 2654208 | tf_op jit(solution)/shard_map/all_gather | solution.py:129
  280.0 2.6 copy-start.4
  281.3 2.5 copy-start.8
  373.1 3.5 copy-start.1
Sparse Core Ops, SparseCore 0:
  11.2 55.3 reduce-scatter.4
  175.0 27.7 reduce-scatter.10
  215.4 27.9 reduce-scatter.8
  246.4 28.5 reduce-scatter.6
  276.6 31.5 all-gather.10
  309.8 30.7 all-gather.8
  342.3 30.7 all-gather.6
